TPU v7x, 128 devices: a whole 4x4x4 slice. The times are simulated.
128 devices in a mesh: ha: 2 (over z_hi), wa: 64 (over y, z_lo, x, core).
Axes of the slice: x: 4, y: 4, z: 4 (z_hi: 2, z_lo: 2; z = z_hi * 2 + z_lo), core: 2. Of those that a mesh axis runs over, the one named last changes fastest.
Arguments:
- queries: float32 [2, 16, 512, 256], P(None, 'ha', 'wa'), may hold values from -240 to 240
- keys: float32 [2, 16, 512, 256], P(None, 'ha', 'wa'), may hold values from -6 to 6
- values: float32 [2, 16, 512, 256], P(None, 'ha', 'wa'), may hold values from -6 to 6
- cotangent: float32 [2, 16, 512, 256], P(None, 'ha', 'wa'), may hold values from -6 to 6
Outputs:
- query_grad: float32 [2, 16, 512, 256], P(None, 'ha', 'wa')
- key_grad: float32 [2, 16, 512, 256], P(None, 'ha', 'wa')
- value_grad: float32 [2, 16, 512, 256], P(None, 'ha', 'wa')
All inputs are finite; a program needn't handle non-finite values.
Results may differ from a plain program's by a relative error of at most 0.0003.
Values sent between devices are 32-bit elements; how exact they have to be, the bound alone decides.
A program may use at most 128 MiB of HBM per device.

v0:
```python
import functools

import jax
import jax.numpy as jnp
from jax import lax
from jax.experimental import pallas as pl
from jax.experimental.pallas import tpu as pltpu
from jax.sharding import PartitionSpec as P

HEADS = 4
REACH = 3
MESH = pl.DeviceIdType.MESH

TILE = 8
TOKENS = 64
EDGE = REACH * TILE
LEFT = 64
RIGHT = 88
WIDE = 112
OWN = 256
SLOTS = 32
LANES = 384
SCALE = 1.0 / 8.0
FAR = -1e30


def dot(a, b, contract):
    return lax.dot_general(a, b, (contract, ((), ())), preferred_element_type=jnp.float32)


def split(x, parts):
    out = []
    for index in range(parts):
        part = x.astype(jnp.bfloat16)
        out.append(part)
        if index + 1 < parts:
            x = x - part.astype(jnp.float32)
    return out


def beside(parts, order):
    return jnp.concatenate([parts[index] for index in order], axis=1)


def below(parts, order):
    return jnp.concatenate([parts[index] for index in order], axis=0)


def product(a, b, order, contract):
    left = beside if contract[0][0] else below
    right = beside if contract[1][0] else below
    return dot(left(a, [i for i, _ in order]), right(b, [j for _, j in order]), contract)


SIX = ((2, 0), (0, 2), (1, 1), (1, 0), (0, 1), (0, 0))
THREE = ((1, 0), (0, 1), (0, 0))


def third(index):
    return (index * 11) >> 5


def kernel(
    wa_count,
    q_hbm,
    k_hbm,
    v_hbm,
    c_hbm,
    dq_ref,
    dk_ref,
    dv_ref,
    kv,
    qc,
    halo,
    packed,
    bias,
    qs,
    cs,
    sheet_out,
    sheet_in,
    terms,
    back,
    part_out,
    part_in,
    load_sem,
    row_sem,
    col_sem,
    sheet_sem,
    term_sem,
    part_sem,
):
    images, tokens, channels = q_hbm.shape
    head_size = channels // HEADS
    ha = lax.axis_index("ha")
    wa = lax.axis_index("wa")
    other = 1 - ha
    has = (wa > 0, wa < wa_count - 1)
    side_device = ((ha, jnp.maximum(wa - 1, 0)), (ha, jnp.minimum(wa + 1, wa_count - 1)))
    partner = (other, wa)

    barrier = pltpu.get_barrier_semaphore()

    def greet(device):
        pl.semaphore_signal(barrier, inc=1, device_id=device, device_id_type=MESH)

    greet(partner)
    for side in range(2):
        pl.when(has[side])(functools.partial(greet, side_device[side]))

    loads = {}
    for name, ref, target in (
        ("k", k_hbm, kv.at[:, 0, pl.ds(0, tokens)]),
        ("v", v_hbm, kv.at[:, 1, pl.ds(0, tokens)]),
        ("q", q_hbm, qc.at[:, 0]),
        ("c", c_hbm, qc.at[:, 1]),
    ):
        loads[name] = pltpu.make_async_copy(ref, target, load_sem.at[len(loads)])
        loads[name].start()

    edge = (TILE - REACH) * other

    def iota(shape, dim):
        return lax.broadcasted_iota(jnp.int32, shape, dim)

    lane = iota((1, LANES), 1)
    slot = jnp.where(lane < OWN, lane & (tokens - 1), lane & (SLOTS - 1))
    own_row = ((slot >> 3) + edge) & (TILE - 1)
    far_row = jnp.where(slot < EDGE, jnp.where(ha == 0, TILE, -REACH) + (slot >> 3), 100)
    query_row = jnp.where(lane < OWN, own_row, far_row)
    query_col = slot & (TILE - 1)
    for first, size in ((0, tokens), (LEFT, EDGE), (RIGHT, EDGE)):
        index = iota((size, 1), 0)
        if first == 0:
            row, col = index >> 3, index & (TILE - 1)
        else:
            row = third(index)
            col = index - 3 * row + (-REACH if first == LEFT else TILE)
            row = row + jnp.where(has[0 if first == LEFT else 1], 0, 1000)
        gap = jnp.maximum(jnp.abs(row - query_row), jnp.abs(col - query_col))
        bias[first : first + size] = jnp.where(gap <= REACH, 0.0, FAR)
    for image in range(images):
        for field in range(2):
            halo[image, field, EDGE:SLOTS] = jnp.zeros((SLOTS - EDGE, channels), jnp.float32)

    def clear(first):
        for image in range(images):
            for field in range(2):
                kv[image, field, first : first + EDGE] = jnp.zeros((EDGE, channels), jnp.float32)

    pl.when(jnp.logical_not(has[0]))(lambda: clear(LEFT))
    pl.when(jnp.logical_not(has[1]))(lambda: clear(RIGHT))

    cut = (slice(0, REACH), slice(TILE - REACH, TILE))
    for field, name in enumerate("kv"):
        loads[name].wait()
        for image in range(images):
            mine = kv[image, field, 0:tokens]
            for row in range(TILE):
                line = mine[row * TILE : (row + 1) * TILE]
                for side in range(2):
                    packed[image, side, field, 3 * row : 3 * row + 3] = line[cut[side]]
    loads["q"].wait()
    loads["c"].wait()

    pl.semaphore_wait(barrier, 1 + has[0].astype(jnp.int32) + has[1].astype(jnp.int32))

    def remote(source, target, sems, index, device):
        return pltpu.make_async_remote_copy(
            src_ref=source,
            dst_ref=target,
            send_sem=sems.at[(0,) + index],
            recv_sem=sems.at[(1,) + index],
            device_id=device,
            device_id_type=MESH,
        )

    edge_start = pl.multiple_of(edge * TILE, TILE)

    def row_copy(image):
        source = qc.at[image, :, pl.ds(edge_start, EDGE)]
        return remote(source, halo.at[image, :, pl.ds(0, EDGE)], row_sem, (image,), partner)

    def col_copy(image, side):
        target = kv.at[image, :, pl.ds((RIGHT, LEFT)[side], EDGE)]
        return remote(packed.at[image, side], target, col_sem, (image, side), side_device[side])

    def sheet_copy(image):
        return remote(sheet_out.at[image], sheet_in.at[image], sheet_sem, (image,), partner)

    def term_copy(image, side):
        source, target = terms.at[image, side], back.at[image, side]
        return remote(source, target, term_sem, (image, side), side_device[side])

    def part_copy(image):
        return remote(part_out.at[image], part_in.at[image], part_sem, (image,), partner)

    for image in range(images):
        row_copy(image).start()
        for side in range(2):
            pl.when(has[side])(col_copy(image, side).start)

    lane_head = iota((tokens, channels), 1) // head_size
    heads = [jnp.where(lane_head == head, 1.0, 0.0).astype(jnp.bfloat16) for head in range(HEADS)]

    def turned(row):
        return pl.ds(pl.multiple_of(((row + edge) & (TILE - 1)) * TILE, TILE), TILE)

    def stack_own(image):
        for field, stack, factor, parts in ((0, qs, SCALE, 3), (1, cs, 1.0, 2)):
            field_rows = [qc[image, field, turned(row)] for row in range(TILE)]
            for index, part in enumerate(split(jnp.concatenate(field_rows, 0) * factor, parts)):
                for head in range(HEADS):
                    stack[image, index, head * tokens : (head + 1) * tokens] = part * heads[head]

    def stack_halo(image):
        for field, stack, factor, parts in ((0, qs, SCALE, 3), (1, cs, 1.0, 2)):
            for index, part in enumerate(split(halo[image, field] * factor, parts)):
                for head in range(HEADS):
                    base = OWN + SLOTS * head
                    stack[image, index, base : base + SLOTS] = part * heads[head][:SLOTS]

    def parts_of(ref, image, count):
        return [ref[image, index] for index in range(count)]

    lane128 = iota((8, 128), 1)

    def to_slots(wide_sheet):
        low, high = wide_sheet[:, :128], wide_sheet[:, 128:]
        out = jnp.where(lane128 < 32, low, pltpu.roll(low, 96, 1))
        out = jnp.where(lane128 < 64, out, pltpu.roll(high, 64, 1))
        return jnp.where(lane128 < 96, out, pltpu.roll(high, 32, 1))

    def from_slots(sheet):
        low = jnp.where(lane128 < 64, sheet, pltpu.roll(sheet, 32, 1))
        high = jnp.where(lane128 < 64, pltpu.roll(sheet, 64, 1), pltpu.roll(sheet, 96, 1))
        return jnp.concatenate([low, high], axis=1)

    def first_pass(image):
        keys = split(kv[image, 0], 3)
        scores = product(keys, parts_of(qs, image, 3), SIX, ((1,), (1,))) + bias[...]
        values = split(kv[image, 1], 2)
        dprobs = product(values, parts_of(cs, image, 2), THREE, ((1,), (1,)))
        top = jnp.max(scores, axis=0, keepdims=True)
        expd = jnp.exp(scores - top)
        mass = jnp.sum(expd, axis=0, keepdims=True)
        moment = jnp.sum(expd * dprobs, axis=0, keepdims=True)
        sheet = jnp.concatenate([top, mass, moment, jnp.zeros((5, LANES), jnp.float32)], axis=0)
        mine = to_slots(sheet[:, :OWN])
        sheet_out[image, 0:3] = mine[0:3]
        sheet_out[image, 3:6] = sheet[0:3, OWN:]
        sheet_out[image, 6:8] = jnp.zeros((2, 128), jnp.float32)
        sheet_copy(image).start()
        return keys, expd, dprobs, top, mass, moment

    def fold(stacked, size):
        total = jnp.zeros((size, channels), jnp.float32)
        for head in range(HEADS):
            total = total + jnp.where(
                lane_head[:size] == head, stacked[head * size : (head + 1) * size], 0.0
            )
        return total

    live_own = (iota((1, OWN), 1) & (tokens - 1)) < EDGE
    live_far = (iota((1, 128), 1) & (SLOTS - 1)) < EDGE

    def second_pass(image, keys, expd, dprobs, top, mass, moment):
        sheet_copy(image).wait_recv()
        sheet = sheet_in[image]
        seen = from_slots(jnp.concatenate([sheet[3:6], jnp.zeros((5, 128), jnp.float32)], 0))
        top_b = jnp.where(live_own, seen[0:1], FAR)
        mass_b = jnp.where(live_own, seen[1:2], 0.0)
        moment_b = jnp.where(live_own, seen[2:3], 0.0)
        top_b = jnp.concatenate([top_b, sheet[0:1]], axis=1)
        mass_b = jnp.concatenate([mass_b, sheet[1:2]], axis=1)
        moment_b = jnp.concatenate([moment_b, sheet[2:3]], axis=1)
        highest = jnp.maximum(top, top_b)
        share_a = jnp.exp(top - highest)
        share_b = jnp.exp(top_b - highest)
        norm = 1.0 / (mass * share_a + mass_b * share_b)
        delta = (moment * share_a + moment_b * share_b) * norm
        factor = share_a * norm
        factor = jnp.concatenate(
            [factor[:, :OWN], jnp.where(live_far, factor[:, OWN:], 0.0)], axis=1
        )
        probs = expd * factor
        dscores = probs * (dprobs - delta)
        dparts = split(dscores, 2)
        dkeys = product(dparts, parts_of(qs, image, 2), THREE, ((1,), (0,)))
        dvalues = product(split(probs, 2), parts_of(cs, image, 2), THREE, ((1,), (0,)))
        for side, first in enumerate((LEFT, RIGHT)):
            terms[image, side, 0] = dkeys[first : first + EDGE]
            terms[image, side, 1] = dvalues[first : first + EDGE]
            pl.when(has[side])(term_copy(image, side).start)
        spread = product(dparts, keys, THREE, ((0,), (0,)))
        part_out[image] = fold(spread[OWN:], SLOTS)[:EDGE] * SCALE
        part_copy(image).start()
        dk_ref[image] = dkeys[:tokens]
        dv_ref[image] = dvalues[:tokens]
        own = fold(spread[:OWN], tokens) * SCALE
        for row in range(TILE):
            dq_ref[image, turned(row)] = own[row * TILE : (row + 1) * TILE]

    for image in range(images):
        stack_own(image)
    kept = []
    for image in range(images):
        row_copy(image).wait_recv()
        stack_halo(image)
        for side in range(2):
            pl.when(has[side])(col_copy(image, 1 - side).wait_recv)
        kept.append(first_pass(image))
    for image in range(images):
        second_pass(image, *kept[image])

    for image in range(images):
        for side in range(2):

            def add(image=image, side=side):
                term_copy(image, 1 - side).wait_recv()
                for field, ref in enumerate((dk_ref, dv_ref)):
                    for row in range(TILE):
                        at = row * TILE + cut[side].start
                        ref[image, at : at + 3] += back[image, 1 - side, field, 3 * row : 3 * row + 3]

            pl.when(has[side])(add)
        part_copy(image).wait_recv()
        dq_ref[image, pl.ds(edge_start, EDGE)] += part_in[image]

    for image in range(images):
        row_copy(image).wait_send()
        sheet_copy(image).wait_send()
        part_copy(image).wait_send()
        for side in range(2):
            pl.when(has[side])(col_copy(image, side).wait_send)
            pl.when(has[side])(term_copy(image, side).wait_send)


def store(*refs):
    sem = refs[6]
    copies = [pltpu.make_async_copy(refs[i], refs[3 + i], sem.at[i]) for i in range(3)]
    for copy in copies:
        copy.start()
    for copy in copies:
        copy.wait()


def per_device(wa_count, queries, keys, values, cotangent):
    images, tile_rows, tile_cols, channels = queries.shape
    flat = (images, tile_rows * tile_cols, channels)
    f32, bf16 = jnp.float32, jnp.bfloat16
    out = jax.ShapeDtypeStruct(flat, f32)
    sems = pltpu.SemaphoreType.DMA
    results = pl.pallas_call(
        functools.partial(kernel, wa_count),
        out_shape=(pltpu.VMEM(flat, f32),) * 3,
        in_specs=[pl.BlockSpec(memory_space=pl.ANY)] * 4,
        out_specs=(pl.BlockSpec(memory_space=pltpu.VMEM),) * 3,
        scratch_shapes=[
            pltpu.VMEM((images, 2, WIDE, channels), f32),
            pltpu.VMEM((images, 2, TOKENS, channels), f32),
            pltpu.VMEM((images, 2, SLOTS, channels), f32),
            pltpu.VMEM((images, 2, 2, EDGE, channels), f32),
            pltpu.VMEM((WIDE, LANES), f32),
            pltpu.VMEM((images, 3, LANES, channels), bf16),
            pltpu.VMEM((images, 2, LANES, channels), bf16),
            pltpu.VMEM((images, 8, 128), f32),
            pltpu.VMEM((images, 8, 128), f32),
            pltpu.VMEM((images, 2, 2, EDGE, channels), f32),
            pltpu.VMEM((images, 2, 2, EDGE, channels), f32),
            pltpu.VMEM((images, EDGE, channels), f32),
            pltpu.VMEM((images, EDGE, channels), f32),
            sems((4,)),
            sems((2, images)),
            sems((2, images, 2)),
            sems((2, images)),
            sems((2, images, 2)),
            sems((2, images)),
        ],
        compiler_params=pltpu.CompilerParams(collective_id=0, has_side_effects=True),
    )(*(x.reshape(flat) for x in (queries, keys, values, cotangent)))
    results = pl.pallas_call(
        store,
        out_shape=(out, out, out),
        in_specs=[pl.BlockSpec(memory_space=pltpu.VMEM)] * 3,
        out_specs=(pl.BlockSpec(memory_space=pl.ANY),) * 3,
        scratch_shapes=[sems((3,))],
    )(*(pltpu.with_memory_space_constraint(x, pltpu.VMEM) for x in results))
    return tuple(x.reshape(queries.shape) for x in results)


def solution(mesh):
    spec = P(None, "ha", "wa", None)
    return jax.shard_map(
        functools.partial(per_device, mesh.shape["wa"]),
        mesh=mesh,
        in_specs=(spec,) * 4,
        out_specs=(spec,) * 3,
        check_vma=False,
    )
```

profile of v0, /device:TPU:24, one launch (start us, length us, event | category | flops | bytes accessed | tf_op | source)
XLA Modules:
  0.0 21.0 jit_solution(7833233682173559190)
XLA Ops:
  0.6 19.5 %shard_map.67 = (f32[2,64,256]{2,1,0:T(8,128)S(1)}, f32[2,64,256]{2,1,0:T(8,128)S(1)}, f32[2,64,256]{2,1,0:T(8,128)S(1)}) custom-call(f32[2,64,256]{2,1,0:T(8,128)} %bitcast.7, f32[2,64,256]{2,1,0:T(8,128)} %bitcast.8, f32[2,64,256]{2,1,0:T(8,128)} %bitcast.9, f32[2,64,256]{2,1,0:T(8,128)} %bitcast.10), custom_call_target="tpu_custom_call" | custom-call | tf_op jit(solution)/shard_map/pallas_call | solution.py:353
  20.2 0.8 %shard_map.68 = (f32[2,64,256]{2,1,0:T(8,128)}, f32[2,64,256]{2,1,0:T(8,128)}, f32[2,64,256]{2,1,0:T(8,128)}) custom-call(f32[2,64,256]{2,1,0:T(8,128)S(1)} %get-tuple-element.9.refs_0_, f32[2,64,256]{2,1,0:T(8,128)S(1)} %get-tuple-element.10.refs_1_, f32[2,64,256]{2,1,0:T(8,128)S(1)} %get-tuple-element.11.refs_2_), custom_call_target="tpu_custom_call" | custom-call | tf_op jit(solution)/shard_map/pallas_call | solution.py:381
where the time goes:
time: 21.1 us; the launch traced here: 21 us
  Pallas kernels  20.3 us (96%)
  between operations  0.64 us (3%)
    pallas_call x1, Pallas kernels, per_device(): pl.pallas_call(functools.partial(kernel, wa_count), out_shape=(pltpu.VMEM...  19.5 us
    pallas_call x1, Pallas kernels, per_device(): pl.pallas_call(store, out_shape=(out, out, out), in_specs=[pl.BlockSpec(m...  0.77 us

commit v1 on v0

--- a/solution.py
+++ b/solution.py
@@ -151,17 +151,19 @@
     pl.when(jnp.logical_not(has[1]))(lambda: clear(RIGHT))
 
     cut = (slice(0, REACH), slice(TILE - REACH, TILE))
-    for field, name in enumerate("kv"):
-        loads[name].wait()
+
+    def pack():
+        for name in "kvqc":
+            loads[name].wait()
         for image in range(images):
-            mine = kv[image, field, 0:tokens]
-            for row in range(TILE):
-                line = mine[row * TILE : (row + 1) * TILE]
-                for side in range(2):
-                    packed[image, side, field, 3 * row : 3 * row + 3] = line[cut[side]]
-    loads["q"].wait()
-    loads["c"].wait()
-
+            for field in range(2):
+                mine = kv[image, field, 0:tokens]
+                for row in range(TILE):
+                    line = mine[row * TILE : (row + 1) * TILE]
+                    for side in range(2):
+                        packed[image, side, field, 3 * row : 3 * row + 3] = line[cut[side]]
+
+    pack()
     pl.semaphore_wait(barrier, 1 + has[0].astype(jnp.int32) + has[1].astype(jnp.int32))
 
     def remote(source, target, sems, index, device):
@@ -184,8 +186,9 @@
         target = kv.at[image, :, pl.ds((RIGHT, LEFT)[side], EDGE)]
         return remote(packed.at[image, side], target, col_sem, (image, side), side_device[side])
 
-    def sheet_copy(image):
-        return remote(sheet_out.at[image], sheet_in.at[image], sheet_sem, (image,), partner)
+    def sheet_copy(image, kind):
+        source, target = sheet_out.at[image, kind], sheet_in.at[image, kind]
+        return remote(source, target, sheet_sem, (image, kind), partner)
 
     def term_copy(image, side):
         source, target = terms.at[image, side], back.at[image, side]
@@ -219,9 +222,6 @@
                     base = OWN + SLOTS * head
                     stack[image, index, base : base + SLOTS] = part * heads[head][:SLOTS]
 
-    def parts_of(ref, image, count):
-        return [ref[image, index] for index in range(count)]
-
     lane128 = iota((8, 128), 1)
 
     def to_slots(wide_sheet):
@@ -235,22 +235,21 @@
         high = jnp.where(lane128 < 64, pltpu.roll(sheet, 64, 1), pltpu.roll(sheet, 96, 1))
         return jnp.concatenate([low, high], axis=1)
 
-    def first_pass(image):
-        keys = split(kv[image, 0], 3)
-        scores = product(keys, parts_of(qs, image, 3), SIX, ((1,), (1,))) + bias[...]
-        values = split(kv[image, 1], 2)
-        dprobs = product(values, parts_of(cs, image, 2), THREE, ((1,), (1,)))
+    def first_pass(image, first, size, keys, values):
+        lanes = slice(first, first + size)
+        stacked = [qs[image, index, lanes] for index in range(3)]
+        scores = product(keys, stacked, SIX, ((1,), (1,))) + bias[:, lanes]
+        stacked = [cs[image, index, lanes] for index in range(2)]
+        dprobs = product(values, stacked, THREE, ((1,), (1,)))
         top = jnp.max(scores, axis=0, keepdims=True)
         expd = jnp.exp(scores - top)
         mass = jnp.sum(expd, axis=0, keepdims=True)
         moment = jnp.sum(expd * dprobs, axis=0, keepdims=True)
-        sheet = jnp.concatenate([top, mass, moment, jnp.zeros((5, LANES), jnp.float32)], axis=0)
-        mine = to_slots(sheet[:, :OWN])
-        sheet_out[image, 0:3] = mine[0:3]
-        sheet_out[image, 3:6] = sheet[0:3, OWN:]
-        sheet_out[image, 6:8] = jnp.zeros((2, 128), jnp.float32)
-        sheet_copy(image).start()
-        return keys, expd, dprobs, top, mass, moment
+        sheet = jnp.concatenate([top, mass, moment, jnp.zeros((5, size), jnp.float32)], axis=0)
+        kind = int(first == OWN)
+        sheet_out[image, kind] = sheet if kind else to_slots(sheet)
+        sheet_copy(image, kind).start()
+        return expd, dprobs, top, mass, moment
 
     def fold(stacked, size):
         total = jnp.zeros((size, channels), jnp.float32)
@@ -263,54 +262,71 @@
     live_own = (iota((1, OWN), 1) & (tokens - 1)) < EDGE
     live_far = (iota((1, 128), 1) & (SLOTS - 1)) < EDGE
 
-    def second_pass(image, keys, expd, dprobs, top, mass, moment):
-        sheet_copy(image).wait_recv()
-        sheet = sheet_in[image]
-        seen = from_slots(jnp.concatenate([sheet[3:6], jnp.zeros((5, 128), jnp.float32)], 0))
-        top_b = jnp.where(live_own, seen[0:1], FAR)
-        mass_b = jnp.where(live_own, seen[1:2], 0.0)
-        moment_b = jnp.where(live_own, seen[2:3], 0.0)
-        top_b = jnp.concatenate([top_b, sheet[0:1]], axis=1)
-        mass_b = jnp.concatenate([mass_b, sheet[1:2]], axis=1)
-        moment_b = jnp.concatenate([moment_b, sheet[2:3]], axis=1)
+    def weights(image, first, size, expd, dprobs, top, mass, moment):
+        kind = int(first != OWN)
+        sheet_copy(image, kind).wait_recv()
+        sheet = sheet_in[image, kind]
+        if kind:
+            sheet = from_slots(sheet)
+            top_b = jnp.where(live_own, sheet[0:1], FAR)
+            mass_b = jnp.where(live_own, sheet[1:2], 0.0)
+            moment_b = jnp.where(live_own, sheet[2:3], 0.0)
+        else:
+            top_b, mass_b, moment_b = sheet[0:1], sheet[1:2], sheet[2:3]
         highest = jnp.maximum(top, top_b)
         share_a = jnp.exp(top - highest)
         share_b = jnp.exp(top_b - highest)
         norm = 1.0 / (mass * share_a + mass_b * share_b)
         delta = (moment * share_a + moment_b * share_b) * norm
         factor = share_a * norm
-        factor = jnp.concatenate(
-            [factor[:, :OWN], jnp.where(live_far, factor[:, OWN:], 0.0)], axis=1
-        )
+        if not kind:
+            factor = jnp.where(live_far, factor, 0.0)
         probs = expd * factor
         dscores = probs * (dprobs - delta)
-        dparts = split(dscores, 2)
-        dkeys = product(dparts, parts_of(qs, image, 2), THREE, ((1,), (0,)))
-        dvalues = product(split(probs, 2), parts_of(cs, image, 2), THREE, ((1,), (0,)))
+        return split(probs, 2), split(dscores, 2)
+
+    def key_terms(image, first, size, probs, dscores):
+        lanes = slice(first, first + size)
+        stacked = [qs[image, index, lanes] for index in range(2)]
+        dkeys = product(dscores, stacked, THREE, ((1,), (0,)))
+        stacked = [cs[image, index, lanes] for index in range(2)]
+        return dkeys, product(probs, stacked, THREE, ((1,), (0,)))
+
+    for image in range(images):
+        stack_own(image)
+    parts, own_kept, far_kept, far_terms, own_grads = [], [], [], [], []
+    for image in range(images):
+        for side in range(2):
+            pl.when(has[side])(col_copy(image, 1 - side).wait_recv)
+        parts.append((split(kv[image, 0], 3), split(kv[image, 1], 2)))
+        own_kept.append(first_pass(image, 0, OWN, *parts[image]))
+    for image in range(images):
+        row_copy(image).wait_recv()
+        stack_halo(image)
+        far_kept.append(first_pass(image, OWN, LANES - OWN, *parts[image]))
+    for image in range(images):
+        far_kept[image] = weights(image, OWN, LANES - OWN, *far_kept[image])
+        spread = product(far_kept[image][1], parts[image][0], THREE, ((0,), (0,)))
+        part_out[image] = fold(spread, SLOTS)[:EDGE] * SCALE
+        part_copy(image).start()
+    for image in range(images):
+        far_terms.append(key_terms(image, OWN, LANES - OWN, *far_kept[image]))
+    for image in range(images):
+        own_kept[image] = weights(image, 0, OWN, *own_kept[image])
+        dkeys, dvalues = key_terms(image, 0, OWN, *own_kept[image])
+        dkeys = dkeys + far_terms[image][0]
+        dvalues = dvalues + far_terms[image][1]
         for side, first in enumerate((LEFT, RIGHT)):
             terms[image, side, 0] = dkeys[first : first + EDGE]
             terms[image, side, 1] = dvalues[first : first + EDGE]
             pl.when(has[side])(term_copy(image, side).start)
-        spread = product(dparts, keys, THREE, ((0,), (0,)))
-        part_out[image] = fold(spread[OWN:], SLOTS)[:EDGE] * SCALE
-        part_copy(image).start()
-        dk_ref[image] = dkeys[:tokens]
-        dv_ref[image] = dvalues[:tokens]
-        own = fold(spread[:OWN], tokens) * SCALE
+        own_grads.append((dkeys[:tokens], dvalues[:tokens]))
+    for image in range(images):
+        dk_ref[image], dv_ref[image] = own_grads[image]
+        spread = product(own_kept[image][1], parts[image][0], THREE, ((0,), (0,)))
+        own = fold(spread, tokens) * SCALE
         for row in range(TILE):
             dq_ref[image, turned(row)] = own[row * TILE : (row + 1) * TILE]
-
-    for image in range(images):
-        stack_own(image)
-    kept = []
-    for image in range(images):
-        row_copy(image).wait_recv()
-        stack_halo(image)
-        for side in range(2):
-            pl.when(has[side])(col_copy(image, 1 - side).wait_recv)
-        kept.append(first_pass(image))
-    for image in range(images):
-        second_pass(image, *kept[image])
 
     for image in range(images):
         for side in range(2):
@@ -328,7 +344,8 @@
 
     for image in range(images):
         row_copy(image).wait_send()
-        sheet_copy(image).wait_send()
+        for kind in range(2):
+            sheet_copy(image, kind).wait_send()
         part_copy(image).wait_send()
         for side in range(2):
             pl.when(has[side])(col_copy(image, side).wait_send)
@@ -363,8 +380,8 @@
             pltpu.VMEM((WIDE, LANES), f32),
             pltpu.VMEM((images, 3, LANES, channels), bf16),
             pltpu.VMEM((images, 2, LANES, channels), bf16),
-            pltpu.VMEM((images, 8, 128), f32),
-            pltpu.VMEM((images, 8, 128), f32),
+            pltpu.VMEM((images, 2, 8, 128), f32),
+            pltpu.VMEM((images, 2, 8, 128), f32),
             pltpu.VMEM((images, 2, 2, EDGE, channels), f32),
             pltpu.VMEM((images, 2, 2, EDGE, channels), f32),
             pltpu.VMEM((images, EDGE, channels), f32),
@@ -372,7 +389,7 @@
             sems((4,)),
             sems((2, images)),
             sems((2, images, 2)),
-            sems((2, images)),
+            sems((2, images, 2)),
             sems((2, images, 2)),
             sems((2, images)),
         ],

time: 21.1 us -> 20.7 us (0.981)
  Pallas kernels: 20.3 us -> 20 us
    pallas_call x1, Pallas kernels: 19.5 us -> 19.2 us  [per_device(): pl.pallas_call(functools.partial(kernel, wa_count), out_shape=(pltpu.VMEM...]
where the time goes in v1:
time: 20.7 us; the launch traced here: 20.6 us
  Pallas kernels  20 us (97%)
  between operations  0.64 us (3%)
    pallas_call x1, Pallas kernels, per_device(): pl.pallas_call(functools.partial(kernel, wa_count), out_shape=(pltpu.VMEM...  19.2 us
    pallas_call x1, Pallas kernels, per_device(): pl.pallas_call(store, out_shape=(out, out, out), in_specs=[pl.BlockSpec(m...  0.77 us

profile of v1, /device:TPU:24, one launch (start us, length us, event | category | flops | bytes accessed | tf_op | source)
XLA Modules:
  0.0 20.6 jit_solution(2575533305580693273)
XLA Ops:
  0.6 19.2 %shard_map.67 = (f32[2,64,256]{2,1,0:T(8,128)S(1)}, f32[2,64,256]{2,1,0:T(8,128)S(1)}, f32[2,64,256]{2,1,0:T(8,128)S(1)}) custom-call(f32[2,64,256]{2,1,0:T(8,128)} %bitcast.7, f32[2,64,256]{2,1,0:T(8,128)} %bitcast.8, f32[2,64,256]{2,1,0:T(8,128)} %bitcast.9, f32[2,64,256]{2,1,0:T(8,128)} %bitcast.10), custom_call_target="tpu_custom_call" | custom-call | tf_op jit(solution)/shard_map/pallas_call | solution.py:370
  19.8 0.8 %shard_map.68 = (f32[2,64,256]{2,1,0:T(8,128)}, f32[2,64,256]{2,1,0:T(8,128)}, f32[2,64,256]{2,1,0:T(8,128)}) custom-call(f32[2,64,256]{2,1,0:T(8,128)S(1)} %get-tuple-element.9.refs_0_, f32[2,64,256]{2,1,0:T(8,128)S(1)} %get-tuple-element.10.refs_1_, f32[2,64,256]{2,1,0:T(8,128)S(1)} %get-tuple-element.11.refs_2_), custom_call_target="tpu_custom_call" | custom-call | tf_op jit(solution)/shard_map/pallas_call | solution.py:398

commit v2 on v1

--- a/solution.py
+++ b/solution.py
@@ -76,6 +76,8 @@
     bias,
     qs,
     cs,
+    qt,
+    ct,
     sheet_out,
     sheet_in,
     terms,
@@ -208,19 +210,31 @@
     def turned(row):
         return pl.ds(pl.multiple_of(((row + edge) & (TILE - 1)) * TILE, TILE), TILE)
 
+    def stack(image, first, blocks):
+        for x, rows, columns, count in ((blocks[0] * SCALE, qs, qt, 3), (blocks[1], cs, ct, 2)):
+            size = x.shape[0]
+            lanes = slice(first, first + HEADS * size)
+            for index, part in enumerate(split(x, 2)):
+                for head in range(HEADS):
+                    base = first + head * size
+                    rows[image, index, base : base + size] = part * heads[head][:size]
+            spread = [jnp.where(lane_head[:size] == head, x, 0.0) for head in range(HEADS)]
+            turned_x = jnp.transpose(jnp.concatenate(spread, axis=0))
+            for index, part in enumerate(split(turned_x, count)):
+                columns[image, index, :, lanes] = part
+
     def stack_own(image):
-        for field, stack, factor, parts in ((0, qs, SCALE, 3), (1, cs, 1.0, 2)):
-            field_rows = [qc[image, field, turned(row)] for row in range(TILE)]
-            for index, part in enumerate(split(jnp.concatenate(field_rows, 0) * factor, parts)):
-                for head in range(HEADS):
-                    stack[image, index, head * tokens : (head + 1) * tokens] = part * heads[head]
+        stack(
+            image,
+            0,
+            [
+                jnp.concatenate([qc[image, field, turned(row)] for row in range(TILE)], axis=0)
+                for field in range(2)
+            ],
+        )
 
     def stack_halo(image):
-        for field, stack, factor, parts in ((0, qs, SCALE, 3), (1, cs, 1.0, 2)):
-            for index, part in enumerate(split(halo[image, field] * factor, parts)):
-                for head in range(HEADS):
-                    base = OWN + SLOTS * head
-                    stack[image, index, base : base + SLOTS] = part * heads[head][:SLOTS]
+        stack(image, OWN, [halo[image, field] for field in range(2)])
 
     lane128 = iota((8, 128), 1)
 
@@ -237,10 +251,10 @@
 
     def first_pass(image, first, size, keys, values):
         lanes = slice(first, first + size)
-        stacked = [qs[image, index, lanes] for index in range(3)]
-        scores = product(keys, stacked, SIX, ((1,), (1,))) + bias[:, lanes]
-        stacked = [cs[image, index, lanes] for index in range(2)]
-        dprobs = product(values, stacked, THREE, ((1,), (1,)))
+        stacked = [qt[image, index, :, lanes] for index in range(3)]
+        scores = product(keys, stacked, SIX, ((1,), (0,))) + bias[:, lanes]
+        stacked = [ct[image, index, :, lanes] for index in range(2)]
+        dprobs = product(values, stacked, THREE, ((1,), (0,)))
         top = jnp.max(scores, axis=0, keepdims=True)
         expd = jnp.exp(scores - top)
         mass = jnp.sum(expd, axis=0, keepdims=True)
@@ -328,19 +342,21 @@
         for row in range(TILE):
             dq_ref[image, turned(row)] = own[row * TILE : (row + 1) * TILE]
 
-    for image in range(images):
-        for side in range(2):
-
-            def add(image=image, side=side):
-                term_copy(image, 1 - side).wait_recv()
-                for field, ref in enumerate((dk_ref, dv_ref)):
-                    for row in range(TILE):
-                        at = row * TILE + cut[side].start
-                        ref[image, at : at + 3] += back[image, 1 - side, field, 3 * row : 3 * row + 3]
-
-            pl.when(has[side])(add)
+    def add(image, side):
+        term_copy(image, 1 - side).wait_recv()
+        for field, ref in enumerate((dk_ref, dv_ref)):
+            for row in range(TILE):
+                at = row * TILE + cut[side].start
+                ref[image, at : at + 3] += back[image, 1 - side, field, 3 * row : 3 * row + 3]
+
+    for image in range(images):
         part_copy(image).wait_recv()
         dq_ref[image, pl.ds(edge_start, EDGE)] += part_in[image]
+    even = lax.rem(wa, 2) == 0
+    for parity, order in ((even, (1, 0)), (jnp.logical_not(even), (0, 1))):
+        for side in order:
+            for image in range(images):
+                pl.when(jnp.logical_and(has[side], parity))(functools.partial(add, image, side))
 
     for image in range(images):
         row_copy(image).wait_send()
@@ -378,8 +394,10 @@
             pltpu.VMEM((images, 2, SLOTS, channels), f32),
             pltpu.VMEM((images, 2, 2, EDGE, channels), f32),
             pltpu.VMEM((WIDE, LANES), f32),
-            pltpu.VMEM((images, 3, LANES, channels), bf16),
             pltpu.VMEM((images, 2, LANES, channels), bf16),
+            pltpu.VMEM((images, 2, LANES, channels), bf16),
+            pltpu.VMEM((images, 3, channels, LANES), bf16),
+            pltpu.VMEM((images, 2, channels, LANES), bf16),
             pltpu.VMEM((images, 2, 8, 128), f32),
             pltpu.VMEM((images, 2, 8, 128), f32),
             pltpu.VMEM((images, 2, 2, EDGE, channels), f32),

time: 20.7 us -> 20.2 us (0.976)
  Pallas kernels: 20 us -> 19.4 us
    pallas_call x1, Pallas kernels: 19.2 us -> 18.7 us  [per_device(): pl.pallas_call(functools.partial(kernel, wa_count), out_shape=(pltpu.VMEM...]
where the time goes in v2:
time: 20.2 us; the launch traced here: 20.1 us
  Pallas kernels  19.4 us (96%)
  between operations  0.64 us (3%)
    pallas_call x1, Pallas kernels, per_device(): pl.pallas_call(functools.partial(kernel, wa_count), out_shape=(pltpu.VMEM...  18.7 us
    pallas_call x1, Pallas kernels, per_device(): pl.pallas_call(store, out_shape=(out, out, out), in_specs=[pl.BlockSpec(m...  0.77 us

profile of v2, /device:TPU:24, one launch (start us, length us, event | category | flops | bytes accessed | tf_op | source)
XLA Modules:
  0.0 20.1 jit_solution(14164966060616105954)
XLA Ops:
  0.6 18.7 %shard_map.67 = (f32[2,64,256]{2,1,0:T(8,128)S(1)}, f32[2,64,256]{2,1,0:T(8,128)S(1)}, f32[2,64,256]{2,1,0:T(8,128)S(1)}) custom-call(f32[2,64,256]{2,1,0:T(8,128)} %bitcast.7, f32[2,64,256]{2,1,0:T(8,128)} %bitcast.8, f32[2,64,256]{2,1,0:T(8,128)} %bitcast.9, f32[2,64,256]{2,1,0:T(8,128)} %bitcast.10), custom_call_target="tpu_custom_call" | custom-call | tf_op jit(solution)/shard_map/pallas_call | solution.py:386
  19.3 0.8 %shard_map.68 = (f32[2,64,256]{2,1,0:T(8,128)}, f32[2,64,256]{2,1,0:T(8,128)}, f32[2,64,256]{2,1,0:T(8,128)}) custom-call(f32[2,64,256]{2,1,0:T(8,128)S(1)} %get-tuple-element.9.refs_0_, f32[2,64,256]{2,1,0:T(8,128)S(1)} %get-tuple-element.10.refs_1_, f32[2,64,256]{2,1,0:T(8,128)S(1)} %get-tuple-element.11.refs_2_), custom_call_target="tpu_custom_call" | custom-call | tf_op jit(solution)/shard_map/pallas_call | solution.py:416

commit v3 on v2

--- a/solution.py
+++ b/solution.py
@@ -18,6 +18,7 @@
 RIGHT = 88
 WIDE = 112
 OWN = 256
+HALF = 128
 SLOTS = 32
 LANES = 384
 SCALE = 1.0 / 8.0
@@ -125,7 +126,8 @@
         return lax.broadcasted_iota(jnp.int32, shape, dim)
 
     lane = iota((1, LANES), 1)
-    slot = jnp.where(lane < OWN, lane & (tokens - 1), lane & (SLOTS - 1))
+    slot = lane & (SLOTS - 1)
+    slot = jnp.where((lane >= HALF) & (lane < OWN), slot + SLOTS, slot)
     own_row = ((slot >> 3) + edge) & (TILE - 1)
     far_row = jnp.where(slot < EDGE, jnp.where(ha == 0, TILE, -REACH) + (slot >> 3), 100)
     query_row = jnp.where(lane < OWN, own_row, far_row)
@@ -224,30 +226,16 @@
                 columns[image, index, :, lanes] = part
 
     def stack_own(image):
-        stack(
-            image,
-            0,
-            [
-                jnp.concatenate([qc[image, field, turned(row)] for row in range(TILE)], axis=0)
+        for half in range(2):
+            lines = range(half * SLOTS // TILE, (half + 1) * SLOTS // TILE)
+            blocks = [
+                jnp.concatenate([qc[image, field, turned(row)] for row in lines], axis=0)
                 for field in range(2)
-            ],
-        )
+            ]
+            stack(image, half * HALF, blocks)
 
     def stack_halo(image):
         stack(image, OWN, [halo[image, field] for field in range(2)])
-
-    lane128 = iota((8, 128), 1)
-
-    def to_slots(wide_sheet):
-        low, high = wide_sheet[:, :128], wide_sheet[:, 128:]
-        out = jnp.where(lane128 < 32, low, pltpu.roll(low, 96, 1))
-        out = jnp.where(lane128 < 64, out, pltpu.roll(high, 64, 1))
-        return jnp.where(lane128 < 96, out, pltpu.roll(high, 32, 1))
-
-    def from_slots(sheet):
-        low = jnp.where(lane128 < 64, sheet, pltpu.roll(sheet, 32, 1))
-        high = jnp.where(lane128 < 64, pltpu.roll(sheet, 64, 1), pltpu.roll(sheet, 96, 1))
-        return jnp.concatenate([low, high], axis=1)
 
     def first_pass(image, first, size, keys, values):
         lanes = slice(first, first + size)
@@ -260,9 +248,10 @@
         mass = jnp.sum(expd, axis=0, keepdims=True)
         moment = jnp.sum(expd * dprobs, axis=0, keepdims=True)
         sheet = jnp.concatenate([top, mass, moment, jnp.zeros((5, size), jnp.float32)], axis=0)
-        kind = int(first == OWN)
-        sheet_out[image, kind] = sheet if kind else to_slots(sheet)
-        sheet_copy(image, kind).start()
+        if first != HALF:
+            kind = int(first == OWN)
+            sheet_out[image, kind] = sheet
+            sheet_copy(image, kind).start()
         return expd, dprobs, top, mass, moment
 
     def fold(stacked, size):
@@ -273,20 +262,18 @@
             )
         return total
 
-    live_own = (iota((1, OWN), 1) & (tokens - 1)) < EDGE
     live_far = (iota((1, 128), 1) & (SLOTS - 1)) < EDGE
 
     def weights(image, first, size, expd, dprobs, top, mass, moment):
         kind = int(first != OWN)
         sheet_copy(image, kind).wait_recv()
         sheet = sheet_in[image, kind]
+        top_b, mass_b, moment_b = sheet[0:1], sheet[1:2], sheet[2:3]
         if kind:
-            sheet = from_slots(sheet)
-            top_b = jnp.where(live_own, sheet[0:1], FAR)
-            mass_b = jnp.where(live_own, sheet[1:2], 0.0)
-            moment_b = jnp.where(live_own, sheet[2:3], 0.0)
-        else:
-            top_b, mass_b, moment_b = sheet[0:1], sheet[1:2], sheet[2:3]
+            blank = jnp.zeros((1, HALF), jnp.float32)
+            top_b = jnp.concatenate([jnp.where(live_far, top_b, FAR), blank + FAR], axis=1)
+            mass_b = jnp.concatenate([jnp.where(live_far, mass_b, 0.0), blank], axis=1)
+            moment_b = jnp.concatenate([jnp.where(live_far, moment_b, 0.0), blank], axis=1)
         highest = jnp.maximum(top, top_b)
         share_a = jnp.exp(top - highest)
         share_b = jnp.exp(top_b - highest)
@@ -313,11 +300,14 @@
         for side in range(2):
             pl.when(has[side])(col_copy(image, 1 - side).wait_recv)
         parts.append((split(kv[image, 0], 3), split(kv[image, 1], 2)))
-        own_kept.append(first_pass(image, 0, OWN, *parts[image]))
+        own_kept.append(first_pass(image, 0, HALF, *parts[image]))
     for image in range(images):
         row_copy(image).wait_recv()
         stack_halo(image)
         far_kept.append(first_pass(image, OWN, LANES - OWN, *parts[image]))
+    for image in range(images):
+        rest = first_pass(image, HALF, HALF, *parts[image])
+        own_kept[image] = [jnp.concatenate(pair, axis=1) for pair in zip(own_kept[image], rest)]
     for image in range(images):
         far_kept[image] = weights(image, OWN, LANES - OWN, *far_kept[image])
         spread = product(far_kept[image][1], parts[image][0], THREE, ((0,), (0,)))
@@ -338,7 +328,8 @@
     for image in range(images):
         dk_ref[image], dv_ref[image] = own_grads[image]
         spread = product(own_kept[image][1], parts[image][0], THREE, ((0,), (0,)))
-        own = fold(spread, tokens) * SCALE
+        own = [fold(spread[:HALF], SLOTS), fold(spread[HALF:], SLOTS)]
+        own = jnp.concatenate(own, axis=0) * SCALE
         for row in range(TILE):
             dq_ref[image, turned(row)] = own[row * TILE : (row + 1) * TILE]
 

time: 20.2 us -> 20.2 us (level)
  no operation moved by 1% of the time
where the time goes in v3:
time: 20.2 us; the launch traced here: 20 us
  Pallas kernels  19.4 us (96%)
  between operations  0.64 us (3%)
    pallas_call x1, Pallas kernels, per_device(): pl.pallas_call(functools.partial(kernel, wa_count), out_shape=(pltpu.VMEM...  18.6 us
    pallas_call x1, Pallas kernels, per_device(): pl.pallas_call(store, out_shape=(out, out, out), in_specs=[pl.BlockSpec(m...  0.77 us

profile of v3, /device:TPU:24, one launch (start us, length us, event | category | flops | bytes accessed | tf_op | source)
XLA Modules:
  0.0 20.0 jit_solution(6611029079003170221)
XLA Ops:
  0.6 18.6 %shard_map.67 = (f32[2,64,256]{2,1,0:T(8,128)S(1)}, f32[2,64,256]{2,1,0:T(8,128)S(1)}, f32[2,64,256]{2,1,0:T(8,128)S(1)}) custom-call(f32[2,64,256]{2,1,0:T(8,128)} %bitcast.7, f32[2,64,256]{2,1,0:T(8,128)} %bitcast.8, f32[2,64,256]{2,1,0:T(8,128)} %bitcast.9, f32[2,64,256]{2,1,0:T(8,128)} %bitcast.10), custom_call_target="tpu_custom_call" | custom-call | tf_op jit(solution)/shard_map/pallas_call | solution.py:377
  19.3 0.8 %shard_map.68 = (f32[2,64,256]{2,1,0:T(8,128)}, f32[2,64,256]{2,1,0:T(8,128)}, f32[2,64,256]{2,1,0:T(8,128)}) custom-call(f32[2,64,256]{2,1,0:T(8,128)S(1)} %get-tuple-element.9.refs_0_, f32[2,64,256]{2,1,0:T(8,128)S(1)} %get-tuple-element.10.refs_1_, f32[2,64,256]{2,1,0:T(8,128)S(1)} %get-tuple-element.11.refs_2_), custom_call_target="tpu_custom_call" | custom-call | tf_op jit(solution)/shard_map/pallas_call | solution.py:407

commit v4 on v3

--- a/solution.py
+++ b/solution.py
@@ -306,13 +306,13 @@
         stack_halo(image)
         far_kept.append(first_pass(image, OWN, LANES - OWN, *parts[image]))
     for image in range(images):
-        rest = first_pass(image, HALF, HALF, *parts[image])
-        own_kept[image] = [jnp.concatenate(pair, axis=1) for pair in zip(own_kept[image], rest)]
-    for image in range(images):
         far_kept[image] = weights(image, OWN, LANES - OWN, *far_kept[image])
         spread = product(far_kept[image][1], parts[image][0], THREE, ((0,), (0,)))
         part_out[image] = fold(spread, SLOTS)[:EDGE] * SCALE
         part_copy(image).start()
+    for image in range(images):
+        rest = first_pass(image, HALF, HALF, *parts[image])
+        own_kept[image] = [jnp.concatenate(pair, axis=1) for pair in zip(own_kept[image], rest)]
     for image in range(images):
         far_terms.append(key_terms(image, OWN, LANES - OWN, *far_kept[image]))
     for image in range(images):

time: 20.2 us -> 20.2 us (level)
  no operation moved by 1% of the time
where the time goes in v4:
time: 20.2 us; the launch traced here: 20 us
  Pallas kernels  19.4 us (96%)
  between operations  0.64 us (3%)
    pallas_call x1, Pallas kernels, per_device(): pl.pallas_call(functools.partial(kernel, wa_count), out_shape=(pltpu.VMEM...  18.6 us
    pallas_call x1, Pallas kernels, per_device(): pl.pallas_call(store, out_shape=(out, out, out), in_specs=[pl.BlockSpec(m...  0.77 us

profile of v4, /device:TPU:24, one launch (start us, length us, event | category | flops | bytes accessed | tf_op | source)
XLA Modules:
  0.0 20.0 jit_solution(6688497909449489023)
XLA Ops:
  0.6 18.6 %shard_map.67 = (f32[2,64,256]{2,1,0:T(8,128)S(1)}, f32[2,64,256]{2,1,0:T(8,128)S(1)}, f32[2,64,256]{2,1,0:T(8,128)S(1)}) custom-call(f32[2,64,256]{2,1,0:T(8,128)} %bitcast.7, f32[2,64,256]{2,1,0:T(8,128)} %bitcast.8, f32[2,64,256]{2,1,0:T(8,128)} %bitcast.9, f32[2,64,256]{2,1,0:T(8,128)} %bitcast.10), custom_call_target="tpu_custom_call" | custom-call | tf_op jit(solution)/shard_map/pallas_call | solution.py:377
  19.3 0.8 %shard_map.68 = (f32[2,64,256]{2,1,0:T(8,128)}, f32[2,64,256]{2,1,0:T(8,128)}, f32[2,64,256]{2,1,0:T(8,128)}) custom-call(f32[2,64,256]{2,1,0:T(8,128)S(1)} %get-tuple-element.9.refs_0_, f32[2,64,256]{2,1,0:T(8,128)S(1)} %get-tuple-element.10.refs_1_, f32[2,64,256]{2,1,0:T(8,128)S(1)} %get-tuple-element.11.refs_2_), custom_call_target="tpu_custom_call" | custom-call | tf_op jit(solution)/shard_map/pallas_call | solution.py:407
